TPU v7x, 32 devices: a whole 2x2x4 slice. The times are simulated.
32 devices in a mesh: prompt: 4 (over y, x), sample: 8 (over z, core).
Axes of the slice: x: 2, y: 2, z: 4, core: 2. Of those that a mesh axis runs over, the one named last changes fastest.
Arguments:
- embeddings: bfloat16 [32, 512, 1024], P(('prompt', 'sample')), parts along dimension 0
- lengths: int32 [32], P(('prompt', 'sample')), parts along dimension 0, may hold values from 32 to 512, as said below
Outputs:
- precision: float32 [32, 8], P(('prompt', 'sample')), parts along dimension 0
- utility: float32 [32], P(('prompt', 'sample')), parts along dimension 0
There are 4 independent parts, one for each index of `prompt`. A program takes and returns all parts, laid end to end along the dimension named above; each array names one. Nothing has to cross between parts.
Inputs may be any that keep to these rules, and one draw needn't show every extreme that they name: `lengths`: some sample of the prompt has exactly 512 tokens.
All inputs are finite; a program needn't handle non-finite values.
Results may differ from a plain program's by a relative error of at most 0.0007.
Values may be sent and summed in bfloat16 or wider, within the bound.
A program may use at most 128 MiB of HBM per device.

v0:
```python
import functools

import jax
import jax.numpy as jnp
from jax import lax
from jax.experimental import pallas as pl
from jax.experimental.pallas import tpu as pltpu
from jax.sharding import PartitionSpec as P

MESH = pl.DeviceIdType.MESH
LOW = -4.0
T = 128


def kernel(chips, slots, len_ref, emb_ref, prec_ref, util_ref, units, relay, lens, rows, cols, res,
           unit_in, relay_in, lens_in, res_in, send, side, pass_on, lens_out, res_out):
    p, s = lax.axis_index("prompt"), lax.axis_index("sample")
    x, y, z, c = p % 2, p // 2, s // 2, s % 2
    flip = (x + y) % 2
    hub_z = jnp.where(flip == 0, 2, 1)
    v = jnp.where(flip == 0, z, chips - 1 - z)
    across = jnp.where(c == 0, p + 1 - 2 * x, p + 2 - 4 * y)
    chunks = units.shape[0]
    is_hub = v == 2
    is_near = v == 1
    f32 = jnp.float32

    def at(prompt, sample):
        return {"prompt": prompt, "sample": sample}

    def copy(src, dst, out_sem, in_sem, where):
        return pltpu.make_async_remote_copy(
            src_ref=src, dst_ref=dst, send_sem=out_sem, recv_sem=in_sem,
            device_id=where, device_id_type=MESH)

    barrier = pltpu.get_barrier_semaphore()

    def greet(prompt, sample):
        pl.semaphore_signal(barrier, inc=1, device_id=at(prompt, sample), device_id_type=MESH)

    @pl.when(is_hub)
    def _():
        for d in range(1, slots):
            greet(p, lax.rem(s + d, slots))
        greet(across, s)
        greet(across, 2 * (chips - 1 - z) + c)

    @pl.when(jnp.logical_not(is_hub))
    def _():
        greet(p, 2 * hub_z)
        greet(p, 2 * hub_z + 1)

    @pl.when(is_near)
    def _():
        greet(across, s)

    lens[s] = jnp.full(lens.shape[1:], len_ref[0], jnp.int32)

    @pl.loop(0, chunks)
    def _(k):
        values = emb_ref[0, pl.ds(pl.multiple_of(k * T, T), T), :].astype(f32)
        norm = jnp.sqrt(jnp.sum(values * values, axis=1, keepdims=True) + 1e-06)
        units[k, s] = (values / norm).astype(units.dtype)

    @pl.when(is_hub)
    def _():
        rows[...] = jnp.full(rows.shape, LOW, f32)
        cols[...] = jnp.full(cols.shape, LOW, f32)
        pl.semaphore_wait(barrier, slots + 1)

    @pl.when(is_near)
    def _():
        pl.semaphore_wait(barrier, 3)

    @pl.when(jnp.logical_not(is_hub | is_near))
    def _():
        pl.semaphore_wait(barrier, 2)

    def own(k):
        return units.at[k, s]

    def straight(k):
        return copy(own(k), own(k), send.at[k], unit_in.at[s, k], at(p, 2 * hub_z + c))

    def detour(k):
        return copy(own(k), relay.at[k], send.at[k], relay_in.at[k], at(across, s))

    def hand_on(k):
        return copy(relay.at[k], units.at[k, s], pass_on.at[k], unit_in.at[s, k],
                    at(across, 2 * (chips - 1 - z) + c))

    def to_side(k, slot):
        return copy(units.at[k, slot], units.at[k, slot], side.at[slot, k], unit_in.at[slot, k],
                    at(p, 2 * z + 1 - c))

    def tell(core, where):
        return copy(lens.at[s], lens.at[s], lens_out.at[core], lens_in.at[s], where)

    far = jnp.logical_not(is_hub | is_near)

    @pl.when(far)
    def _():
        for k in range(chunks):
            straight(k).start()

    @pl.when(is_near)
    def _():
        for k in range(chunks):
            detour(k).start()

    @pl.when(jnp.logical_not(is_hub))
    def _():
        for core in range(2):
            tell(core, at(p, 2 * hub_z + core)).start()

    @pl.when(is_hub)
    def _():
        tell(0, at(p, 2 * z + 1 - c)).start()
        for k in range(chunks):
            to_side(k, s).start()

        def step(k):
            return 2 * lax.rem(z + k, chips)

        def others(k):
            return [step(d) + c for d in range(1, chips)]

        hand_wait = lambda k: copy(relay.at[k], relay.at[k], pass_on.at[k], relay_in.at[k],
                                   at(p, 2 * z + 1 - c)).wait_recv()
        for k in range(chunks):
            hand_wait(k)
            hand_on(k).start()
        for d in range(1, slots):
            other = lax.rem(s + d, slots)
            copy(lens.at[other], lens.at[other], lens_out.at[0], lens_in.at[other],
                 at(p, 2 * z + 1 - c)).wait_recv()

        lane = lax.broadcasted_iota(jnp.int32, (1, T), 1)
        lane8 = lax.broadcasted_iota(jnp.int32, (T, T), 1)
        sub = lax.broadcasted_iota(jnp.int32, (T, T), 0)
        high = f32(4.0)

        def col_cap(k, slot):
            return jnp.where(lane + k * T < lens[slot, 0:1, :], high, f32(LOW))

        def row_cap(k, slot):
            return jnp.where(sub + k * T < lens[slot, 0:1, :], high, f32(LOW))

        def group(k, g):
            return units[k, pl.ds(2 * g, 2)].reshape(2 * T, units.shape[3])

        def against(k, g, h, js, keep):
            new = group(k, g)
            best = [[None, None], [None, None]]
            caps = [row_cap(k, 2 * g + q) for q in range(2)]
            for j in js:
                similar = lax.dot_general(new, group(j, h), (((1,), (1,)), ((), ())),
                                          preferred_element_type=f32)
                for w in range(2):
                    cap = col_cap(j, 2 * h + w)
                    for q in range(2):
                        part = similar[q * T:(q + 1) * T, w * T:(w + 1) * T]
                        m = jnp.minimum(part, cap)
                        best[q][w] = m if best[q][w] is None else jnp.maximum(best[q][w], m)
                        if keep(j):
                            n = jnp.max(jnp.minimum(part, caps[q]), axis=0, keepdims=True)
                            at_row = (2 * h + w) * slots + 2 * g + q
                            cols[j, pl.ds(at_row, 1), :] = jnp.maximum(cols[j, pl.ds(at_row, 1), :], n)
            table = rows[k]
            for q in range(2):
                for w in range(2):
                    top = jnp.max(best[q][w], axis=1, keepdims=True)
                    table = jnp.where(lane8 == (2 * g + q) * slots + 2 * h + w, top, table)
            rows[k] = table

        def share_out(k):
            for slot in others(k):
                to_side(k, slot).wait_recv()
                to_side(k, slot).start()

        share_out(0)
        for k in range(chunks):
            if k + 1 < chunks:
                share_out(k + 1)
            for d in range(chips):
                to_side(k, step(d) + 1 - c).wait_recv()

            @pl.loop(0, chips - 1, unroll=True)
            def _(i):
                g = jnp.where(c == 0, i, lax.rem(3 * i + 2, chips + 1))
                h = jnp.where(c == 0, i + 1, lax.rem(3 * i + 5, chips + 1))
                against(k, g, h, range(k + 1), lambda j: True)
                if k:
                    against(k, h, g, range(k), lambda j: True)

            @pl.loop(0, 2, unroll=True)
            def _(i):
                g = 2 * c + i
                against(k, g, g, range(k + 1), lambda j: j < k)

        pair = slots * slots
        total = jnp.zeros((pair, 1), f32)
        own_len = jnp.concatenate([lens[a] for a in range(slots)], axis=0)
        for k in range(chunks):
            best = jnp.maximum(rows[k].T[:pair], cols[k, :pair])
            ok = (lax.broadcasted_iota(jnp.int32, (pair, T), 1) + k * T < own_len) & (best > -3.5)
            total += jnp.sum(jnp.where(ok, best, f32(0.0)), axis=1, keepdims=True)
        share = total / own_len.astype(f32)
        place = lax.broadcasted_iota(jnp.int32, (pair, T), 0) % slots
        spread = jnp.where(lax.broadcasted_iota(jnp.int32, (pair, T), 1) == place, share, f32(0.0))
        res[c] = jnp.sum(spread.reshape(slots, slots, T), axis=1)
        for d in range(1, slots):
            copy(res.at[c], res.at[c], res_out.at[d], res_in.at[c], at(p, lax.rem(s + d, slots))).start()
        for k in range(chunks):
            hand_on(k).wait_send()
            for d in range(chips):
                to_side(k, step(d) + c).wait_send()
        tell(0, at(p, 2 * z + 1 - c)).wait_send()
        copy(res.at[1 - c], res.at[1 - c], res_out.at[0], res_in.at[1 - c], at(p, 2 * z + 1 - c)).wait_recv()

    @pl.when(jnp.logical_not(is_hub))
    def _():
        for k in range(chunks):
            straight(k).wait_send()
        for core in range(2):
            tell(core, at(p, 2 * hub_z + core)).wait_send()
        for core in range(2):
            copy(res.at[core], res.at[core], res_out.at[0], res_in.at[core],
                 at(p, 2 * hub_z + core)).wait_recv()

    whole = res[0] + res[1]
    first = lax.broadcasted_iota(jnp.int32, (slots, T), 0)
    second = lax.broadcasted_iota(jnp.int32, (slots, T), 1)
    row = jnp.sum(jnp.where(first == s, whole, f32(0.0)), axis=0, keepdims=True)
    prec_ref[...] = row[:, :slots]
    mine = ((first == s) | (second == s)) & (first != second)
    both = jnp.sum(jnp.where(mine, whole, f32(0.0)), axis=0, keepdims=True)
    util_ref[...] = jnp.sum(both, axis=1, keepdims=True) / f32(2 * (slots - 1))

    @pl.when(is_hub)
    def _():
        for d in range(1, slots):
            copy(res.at[c], res.at[c], res_out.at[d], res_in.at[c], at(p, lax.rem(s + d, slots))).wait_send()


def fused(slots, embeddings, lengths):
    length, width = embeddings.shape[1:]
    chunks = length // T
    dma = pltpu.SemaphoreType.DMA
    precision, utility = pl.pallas_call(
        functools.partial(kernel, slots // 2, slots),
        out_shape=(jax.ShapeDtypeStruct((1, slots), jnp.float32), jax.ShapeDtypeStruct((1, 1), jnp.float32)),
        in_specs=[pl.BlockSpec(memory_space=pltpu.SMEM), pl.BlockSpec(memory_space=pltpu.VMEM)],
        out_specs=(pl.BlockSpec(memory_space=pltpu.VMEM), pl.BlockSpec(memory_space=pltpu.VMEM)),
        scratch_shapes=[
            pltpu.VMEM((chunks, slots, T, width), jnp.bfloat16),
            pltpu.VMEM((chunks, T, width), jnp.bfloat16),
            pltpu.VMEM((slots, 8, T), jnp.int32),
            pltpu.VMEM((chunks, T, T), jnp.float32),
            pltpu.VMEM((chunks, slots * slots, T), jnp.float32),
            pltpu.VMEM((2, slots, T), jnp.float32),
            dma((slots, chunks)), dma((chunks,)), dma((slots,)), dma((2,)),
            dma((chunks,)), dma((slots, chunks)), dma((chunks,)), dma((2,)), dma((slots,)),
        ],
        compiler_params=pltpu.CompilerParams(collective_id=0, has_side_effects=True),
    )(lengths, embeddings)
    return precision, utility[:, 0]


def tile_pairs(own, own_len, other, other_len):
    similar = jnp.einsum("aie,bje->abij", own, other, preferred_element_type=jnp.float32)
    places = jnp.arange(own.shape[1], dtype=jnp.int32)
    own_ok = places[None, :] < own_len[:, None]
    other_ok = places[None, :] < other_len[:, None]
    masked = jnp.where(other_ok[None, :, None, :], similar, jnp.float32(-4.0))
    best_row = jnp.max(masked, axis=3)
    forward = jnp.sum(jnp.where(own_ok[:, None, :], best_row, jnp.float32(0.0)), axis=2)
    forward = forward / own_len[:, None].astype(jnp.float32)
    masked_col = jnp.where(own_ok[:, None, :, None], similar, jnp.float32(-4.0))
    best_col = jnp.max(masked_col, axis=2)
    backward = jnp.sum(jnp.where(other_ok[None, :, :], best_col, jnp.float32(0.0)), axis=2)
    backward = backward / other_len[None, :].astype(jnp.float32)
    return (forward, backward)


def body(embeddings, lengths):
    values = embeddings.astype(jnp.float32)
    unit = (values / jnp.sqrt(jnp.sum(values * values, axis=2, keepdims=True) + 1e-06)).astype(
        jnp.bfloat16
    )
    devices = lax.axis_size("sample")
    here = lax.axis_index("sample")
    per_dev = unit.shape[0]
    total = per_dev * devices
    base = here * per_dev
    piece = lax.all_gather(unit, "sample", axis=0, tiled=True)
    piece_len = lax.all_gather(lengths, "sample", axis=0, tiled=True)
    ahead, behind = tile_pairs(unit, lengths, piece, piece_len)
    own_index = base + jnp.arange(per_dev, dtype=jnp.int32)
    offdiag = jnp.arange(total, dtype=jnp.int32)[None, :] != own_index[:, None]
    utility = jnp.sum(jnp.where(offdiag, ahead + behind, jnp.float32(0.0)), axis=1)
    utility = utility / jnp.float32(2 * (total - 1))
    return (ahead, utility)


def solution(mesh):
    in_specs = (P(("prompt", "sample"), None, None), P(("prompt", "sample")))
    out_specs = (P(("prompt", "sample"), None), P(("prompt", "sample")))

    def run(embeddings, lengths):
        slots = mesh.shape["sample"]
        if mesh.shape["prompt"] == 4 and slots == 8 and embeddings.shape[0] == 1 and embeddings.shape[1] % T == 0:
            return fused(slots, embeddings, lengths)
        return body(embeddings, lengths)

    return jax.shard_map(run, mesh=mesh, in_specs=in_specs, out_specs=out_specs, check_vma=False)
```

profile of v0, /device:TPU:0, one launch (start us, length us, event | category | flops | bytes accessed | tf_op | source)
XLA Modules:
  0.0 52.7 jit_solution(15796290046690470150)
XLA Ops:
  1.3 48.5 %shard_map.41 = (f32[1,8]{1,0:T(1,128)}, f32[1,1]{1,0:T(1,128)}) custom-call(s32[1]{0:T(128)S(6)} %copy.6.len_ref, bf16[1,512,1024]{2,1,0:T(8,128)(2,1)} %emb_ref.1), custom_call_target="tpu_custom_call" | custom-call | tf_op jit(solution)/shard_map/pallas_call | solution.py:250
  49.8 0.0 copy-start
  49.8 0.6 %copy-done = f32[1,8]{1,0:T(1,128)S(1)} copy-done((f32[1,8]{1,0:T(1,128)S(1)}, f32[1,8]{1,0:T(1,128)}, u32[]{:S(2)}) %copy-start) | copy-done | bytes 56
  50.4 0.5 copy.7
Async XLA Ops:
  49.8 0.6 %copy-start = (f32[1,8]{1,0:T(1,128)S(1)}, f32[1,8]{1,0:T(1,128)}, u32[]{:S(2)}) copy-start(f32[1,8]{1,0:T(1,128)} %get-tuple-element.8) | copy-start | bytes 100
where the time goes:
time: 52.9 us; the launch traced here: 52.7 us
  Pallas kernels  48.5 us (92%)
  between operations  3.05 us (6%)
  local copies, waits for them, and re-layouts  1.13 us (2%)
    pallas_call x1, Pallas kernels, fused(): pl.pallas_call(functools.partial(kernel, slots // 2, slots), out_shape=(j...  48.5 us
    unnamed x3, local copies, waits for them, and re-layouts  1.13 us

commit v1 on v0

v1 whole, which is shorter than its diff:
```python
import functools

import jax
import jax.numpy as jnp
from jax import lax
from jax.experimental import pallas as pl
from jax.experimental.pallas import tpu as pltpu
from jax.sharding import PartitionSpec as P

MESH = pl.DeviceIdType.MESH
T = 128
FIRST = (32, 32, 64)


def pieces_of(length):
    sizes = list(FIRST) + [T] * (length // T - sum(FIRST) // T)
    return [(sum(sizes[:i]), n) for i, n in enumerate(sizes)]


def kernel(chips, slots, emb_ref, len_ref, out_ref, stage, own, left, right, relay, count, lens, rows, cols, pair, res,
           load, main_out, side_out, own_out, own_in, left_in, late_in, relay_in, relay_out, right_in, right_out,
           lens_out, lens_in, res_out, res_in):
    p, s = lax.axis_index("prompt"), lax.axis_index("sample")
    x, y, z, c = p % 2, p // 2, s // 2, s % 2
    flip = (x + y) % 2
    v = jnp.where(flip == 0, z, chips - 1 - z)
    across = jnp.where(c == 0, p + 1 - 2 * x, p + 2 - 4 * y)
    length, width = own.shape[1:]
    chunks = length // T
    halves = length // (2 * T)
    pieces = pieces_of(length)
    sib = 2 * z + 1 - c
    is_far, is_near, is_hub, is_end = v == 0, v == 1, v == 2, v == 3
    f32 = jnp.float32

    def sample(place, core):
        return 2 * jnp.where(flip == 0, place, chips - 1 - place) + core

    def at(prompt, who):
        return {"prompt": prompt, "sample": who}

    def copy(src, dst, out_sem, in_sem, where):
        return pltpu.make_async_remote_copy(
            src_ref=src, dst_ref=dst, send_sem=out_sem, recv_sem=in_sem,
            device_id=where, device_id_type=MESH)

    def chunk(k):
        return pl.ds(k * T, T)

    far, near, hub, end = (sample(i, c) for i in range(chips))
    hub_other, end_other = sample(2, 1 - c), sample(3, 1 - c)
    twin = at(across, 2 * (chips - 1 - z) + c)

    barrier = pltpu.get_barrier_semaphore()

    def greet(where):
        pl.semaphore_signal(barrier, inc=1, device_id=where, device_id_type=MESH)

    greet(at(p, sib))

    @pl.when(is_far)
    def _():
        greet(at(p, near))
        greet(at(p, hub))

    @pl.when(is_near)
    def _():
        greet(at(p, far))
        greet(at(p, hub))

    @pl.when(is_hub)
    def _():
        greet(at(across, s))
        greet(at(p, near))
        greet(at(p, far))
        greet(at(p, end))
        greet(at(p, end_other))
        greet(twin)

    @pl.when(is_end)
    def _():
        greet(at(p, hub))
        greet(at(p, hub_other))

    def fetch(k):
        return pltpu.make_async_copy(emb_ref.at[0, chunk(k)], stage.at[k], load.at[k])

    fetch_len = pltpu.make_async_copy(len_ref, count, load.at[chunks])
    fetch_len.start()
    for k in range(chunks):
        fetch(k).start()
    fetch_len.wait()
    mine = count[0]
    lens[s] = jnp.full(lens.shape[1:], mine, jnp.int32)
    token = lax.broadcasted_iota(jnp.int32, (T, 1), 0)
    first = None
    for k in range(chunks):
        fetch(k).wait()
        values = stage[k].astype(f32)
        unit = values * (1.0 / jnp.sqrt(jnp.sum(values * values, axis=1, keepdims=True) + 1e-06))
        first = unit[0:1] if first is None else first
        own[0, k * T:(k + 1) * T] = jnp.where(token + k * T < mine, unit, first).astype(own.dtype)

    def straight(k):
        return copy(own.at[0, chunk(k)], left.at[k, 0], main_out.at[k], left_in.at[k], at(p, hub))

    def inward(k):
        return copy(own.at[0, chunk(k)], right.at[k, 0], main_out.at[k], right_in.at[0, k], at(p, hub))

    def detour(i):
        lo, n = pieces[i]
        return copy(own.at[0, pl.ds(lo, n)], relay.at[pl.ds(lo, n)], main_out.at[i], relay_in.at[i], at(across, s))

    def hand_on(i):
        lo, n = pieces[i]
        return copy(relay.at[pl.ds(lo, n)], left.at[lo // T, 1, pl.ds(lo % T, n)], relay_out.at[i], late_in.at[i], twin)

    def outward(k, who):
        return copy(own.at[0, chunk(k)], left.at[k, 0], side_out.at[k], left_in.at[k], at(p, who))

    def to_side(k):
        return copy(right.at[k, 0], right.at[k, 1], right_out.at[k], right_in.at[1, k], at(p, sib))

    def tell(i, who):
        return copy(lens.at[s], lens.at[s], lens_out.at[i], lens_in.at[s], at(p, who))

    def told(who):
        copy(lens.at[who], lens.at[who], lens_out.at[0], lens_in.at[who], at(p, sib)).wait_recv()

    def report(i, slot, who):
        return copy(res.at[0], res.at[slot], res_out.at[i], res_in.at[slot], at(p, who))

    share = copy(own.at[0], own.at[1], own_out, own_in, at(p, sib))

    @pl.when(is_far)
    def _():
        pl.semaphore_wait(barrier, 3)
        for k in range(chunks):
            straight(k).start()
        tell(1, hub).start()

    @pl.when(is_near)
    def _():
        pl.semaphore_wait(barrier, 4)
        for i in range(len(pieces)):
            detour(i).start()
        for k in range(chunks):
            outward(k, far).start()
        tell(1, hub).start()
        tell(2, far).start()

    @pl.when(is_hub)
    def _():
        pl.semaphore_wait(barrier, 6)
        for k in range(chunks):
            outward(k, end).start()
        tell(1, end).start()

    @pl.when(is_end)
    def _():
        pl.semaphore_wait(barrier, 3)
        for k in range(chunks):
            inward(k).start()
        tell(1, hub).start()
        tell(2, hub_other).start()

    share.start()
    tell(0, sib).start()

    def pass_on(i):
        hand_wait = copy(relay.at[pl.ds(*pieces[i])], relay.at[pl.ds(*pieces[i])], relay_out.at[i], relay_in.at[i], twin)
        hand_wait.wait_recv()
        hand_on(i).start()

    @pl.when(is_hub)
    def _():
        for i in range(len(FIRST) - 1):
            pass_on(i)

    def dot(a, b):
        return lax.dot_general(a, b, (((1,), (1,)), ((), ())), preferred_element_type=f32)

    def fold(old, new):
        return new if old is None else jnp.maximum(old, new)

    def plus(old, new):
        return new if old is None else old + new

    def down(part):
        return jnp.max(part.reshape(part.shape[0] // 8, 8, part.shape[1]), axis=0)

    def length_of(who):
        return lens[who, 0:1, 0:1]

    def row_sum(best, start, who):
        top = jnp.max(best, axis=1, keepdims=True)
        place = lax.broadcasted_iota(jnp.int32, top.shape, 0) + start
        kept = jnp.where(place < length_of(who), top, f32(0.0))
        return jnp.sum(kept.reshape(top.shape[0] // 8, 8, 1), axis=0)

    def col_sum(best, start, who):
        top = jnp.max(best, axis=0, keepdims=True)
        place = lax.broadcasted_iota(jnp.int32, top.shape, 1) + start
        return jnp.where(place < length_of(who), top, f32(0.0))

    high = lax.broadcasted_iota(jnp.int32, (slots, T), 0)
    wide = lax.broadcasted_iota(jnp.int32, (slots, T), 1)

    def put(table, of, against, total):
        value = jnp.sum(jnp.sum(total, axis=0, keepdims=True), axis=1, keepdims=True)
        value = value / length_of(of).astype(f32)
        return jnp.where((high == of) & (wide == against), value, table)

    ours = [s, sib]
    share.wait_recv()
    told(sib)
    by_row = [None] * halves
    by_col = [None, None]
    for h in range(halves):
        y_side = own[0, 2 * T * h:2 * T * (h + 1)]
        best = [None, None]
        for b in range(2):
            for g in range(halves):
                part = dot(own[b, 2 * T * g:2 * T * (g + 1)], y_side)
                best[b] = fold(best[b], down(part))
                if b == 1:
                    by_row[g] = fold(by_row[g], jnp.maximum(part[:, :T], part[:, T:]))
        for b in range(2):
            by_col[b] = plus(by_col[b], col_sum(best[b], 2 * T * h, s))
    table = jnp.zeros((slots, T), f32)
    for b in range(2):
        table = put(table, s, ours[b], by_col[b])
    total = None
    for g in range(halves):
        total = plus(total, row_sum(by_row[g], 2 * T * g, sib))
    pair[...] = put(table, sib, s, total)

    def align(ids, others, ready, steps):
        n = len(ids)
        sums = {}
        for k in range(chunks):
            last = k == chunks - 1
            steps(k)

            def meet(part, r, new, segments):
                parts = [part[:, a * T:(a + 1) * T] for a in range(n)]
                for a in range(n):
                    best = parts[a] if new else jnp.maximum(rows[r, :, a * T:(a + 1) * T], parts[a])
                    if not last:
                        rows[r, :, a * T:(a + 1) * T] = best
                        continue
                    for lo, size, start, who, key in segments:
                        add = row_sum(best[lo:lo + size], start, who)
                        sums[key, a] = plus(sums.get((key, a)), add)

            if others:
                x_side = right[k].reshape(2 * T, width)
                r = 2 * halves + k
                for j in range(k):
                    part = dot(x_side, left[j].reshape(2 * T, width))
                    for b in range(2):
                        cols[j, 2 + b] = jnp.maximum(cols[j, 2 + b], down(part[b * T:(b + 1) * T]))
                    rows[r] = part if j == 0 else jnp.maximum(rows[r], part)
            ready(k)
            y_side = left[k, :n].reshape(n * T, width)
            best = [None] * 4
            for b in range(2):
                for h in range(halves):
                    part = dot(own[b, 2 * T * h:2 * T * (h + 1)], y_side)
                    best[b] = fold(best[b], down(part))
                    meet(part, b * halves + h, k == 0, [(0, 2 * T, 2 * T * h, ours[b], ours_key(b))])
            if others:
                for j in range(k + 1):
                    part = dot(right[j].reshape(2 * T, width), y_side)
                    for b in range(2):
                        best[2 + b] = fold(best[2 + b], down(part[b * T:(b + 1) * T]))
                    meet(part, 2 * halves + j, k == 0,
                         [(b * T, T, j * T, others[b], 2 + b) for b in range(2)])
            for b in range(4 if others else 2):
                cols[k, b, :, :n * T] = best[b]
        table = jnp.zeros((slots, T), f32)
        whose = ours + list(others)
        for b in range(len(whose)):
            for a in range(n):
                across_sum = None
                for k in range(chunks):
                    across_sum = plus(across_sum, col_sum(cols[k, b, :, a * T:(a + 1) * T], k * T, ids[a]))
                table = put(table, ids[a], whose[b], across_sum)
                table = put(table, whose[b], ids[a], sums[b, a])
        res[0] = table

    def ours_key(b):
        return b

    def arrived(k):
        copy(left.at[k, 0], left.at[k, 0], main_out.at[k], left_in.at[k], at(p, hub)).wait_recv()

    @pl.when(is_hub)
    def _():
        ids = [far, near]
        others = [end, end_other]

        def steps(k):
            if k == 0:
                for who in ids + others:
                    told(who)
                for i in range(len(FIRST) - 1, len(FIRST) + 1):
                    pass_on(i)
            elif len(FIRST) + k < len(pieces):
                pass_on(len(FIRST) + k)
            copy(right.at[k, 0], right.at[k, 0], right_out.at[k], right_in.at[0, k], at(p, sib)).wait_recv()
            to_side(k).start()
            to_side(k).wait_recv()

        def ready(k):
            arrived(k)
            for i, (lo, n) in enumerate(pieces):
                if lo // T == k:
                    hand_on(i).wait_recv()

        align(ids, others, ready, steps)
        report(0, 1, sib).start()
        report(1, 2, far).start()
        report(2, 2, near).start()
        report(3, 2, end).start()
        report(4, 3, end_other).start()

    @pl.when(is_far | is_end)
    def _():
        who = jnp.where(is_far, near, hub)

        def steps(k):
            if k == 0:
                told(who)

        align([who], [], arrived, steps)
        report(0, 1, sib).start()
        report(1, 3, who).start()

    def reported(slot):
        copy(res.at[slot], res.at[slot], res_out.at[0], res_in.at[slot], at(p, sib)).wait_recv()

    @pl.when(is_near)
    def _():
        res[0] = jnp.zeros(res.shape[1:], f32)
        res[1] = jnp.zeros(res.shape[1:], f32)
        for i in range(len(pieces)):
            detour(i).wait_send()
        for k in range(chunks):
            outward(k, far).wait_send()
        tell(1, hub).wait_send()
        tell(2, far).wait_send()
        reported(3)
        reported(2)

    @pl.when(is_far)
    def _():
        res[3] = jnp.zeros(res.shape[1:], f32)
        for k in range(chunks):
            straight(k).wait_send()
        tell(1, hub).wait_send()
        report(0, 1, sib).wait_send()
        report(1, 3, near).wait_send()
        reported(1)
        reported(2)

    @pl.when(is_hub)
    def _():
        res[2] = jnp.zeros(res.shape[1:], f32)
        for k in range(chunks):
            outward(k, end).wait_send()
            to_side(k).wait_send()
        for i in range(len(pieces)):
            hand_on(i).wait_send()
        tell(1, end).wait_send()
        reported(3)
        reported(1)

    @pl.when(is_end)
    def _():
        for k in range(chunks):
            inward(k).wait_send()
        tell(1, hub).wait_send()
        tell(2, hub_other).wait_send()
        report(0, 1, sib).wait_send()
        report(1, 3, hub).wait_send()
        for slot in range(1, 4):
            reported(slot)

    whole = pair[...] + res[0] + res[1] + res[2] + res[3]
    row = jnp.sum(jnp.where(high == s, whole, f32(0.0)), axis=0, keepdims=True)
    mine_too = ((high == s) | (wide == s)) & (high != wide)
    both = jnp.sum(jnp.where(mine_too, whole, f32(0.0)), axis=0, keepdims=True)
    score = jnp.sum(both, axis=1, keepdims=True) / f32(2 * (slots - 1))
    out_ref[...] = jnp.where(high == 0, row, score)
    share.wait_send()
    tell(0, sib).wait_send()

    @pl.when(is_hub)
    def _():
        report(0, 1, sib).wait_send()
        report(1, 2, far).wait_send()
        report(2, 2, near).wait_send()
        report(3, 2, end).wait_send()
        report(4, 3, end_other).wait_send()


def finish(found_ref, precision_ref, utility_ref):
    precision_ref[...] = found_ref[0:1, :precision_ref.shape[1]]
    utility_ref[...] = found_ref[1:2, 0:1]


def fused(slots, embeddings, lengths):
    length, width = embeddings.shape[1:]
    chunks = length // T
    count = len(pieces_of(length))
    dma = pltpu.SemaphoreType.DMA
    vmem = pl.BlockSpec(memory_space=pltpu.VMEM)
    away = pl.BlockSpec(memory_space=pl.ANY)
    found = pl.pallas_call(
        functools.partial(kernel, slots // 2, slots),
        out_shape=jax.ShapeDtypeStruct((slots, T), jnp.float32),
        in_specs=[away, away],
        out_specs=vmem,
        scratch_shapes=[
            pltpu.VMEM((chunks, T, width), jnp.bfloat16),
            pltpu.VMEM((2, length, width), jnp.bfloat16),
            pltpu.VMEM((chunks, 2, T, width), jnp.bfloat16),
            pltpu.VMEM((chunks, 2, T, width), jnp.bfloat16),
            pltpu.VMEM((length, width), jnp.bfloat16),
            pltpu.SMEM((1,), jnp.int32),
            pltpu.VMEM((slots, 8, T), jnp.int32),
            pltpu.VMEM((2 * chunks, 2 * T, 2 * T), jnp.float32),
            pltpu.VMEM((chunks, 4, 8, 2 * T), jnp.float32),
            pltpu.VMEM((slots, T), jnp.float32),
            pltpu.VMEM((4, slots, T), jnp.float32),
            dma((chunks + 1,)), dma((count,)), dma((chunks,)), dma(()), dma(()), dma((chunks,)), dma((count,)),
            dma((count,)), dma((count,)), dma((2, chunks)), dma((chunks,)),
            dma((3,)), dma((slots,)), dma((5,)), dma((4,)),
        ],
        compiler_params=pltpu.CompilerParams(collective_id=0, has_side_effects=True),
    )(embeddings, lengths)
    precision, utility = pl.pallas_call(
        finish,
        out_shape=(jax.ShapeDtypeStruct((1, slots), jnp.float32), jax.ShapeDtypeStruct((1, 1), jnp.float32)),
        in_specs=[vmem],
        out_specs=(vmem, vmem),
    )(found)
    return precision, utility[:, 0]


def tile_pairs(own, own_len, other, other_len):
    similar = jnp.einsum("aie,bje->abij", own, other, preferred_element_type=jnp.float32)
    places = jnp.arange(own.shape[1], dtype=jnp.int32)
    own_ok = places[None, :] < own_len[:, None]
    other_ok = places[None, :] < other_len[:, None]
    masked = jnp.where(other_ok[None, :, None, :], similar, jnp.float32(-4.0))
    best_row = jnp.max(masked, axis=3)
    forward = jnp.sum(jnp.where(own_ok[:, None, :], best_row, jnp.float32(0.0)), axis=2)
    forward = forward / own_len[:, None].astype(jnp.float32)
    masked_col = jnp.where(own_ok[:, None, :, None], similar, jnp.float32(-4.0))
    best_col = jnp.max(masked_col, axis=2)
    backward = jnp.sum(jnp.where(other_ok[None, :, :], best_col, jnp.float32(0.0)), axis=2)
    backward = backward / other_len[None, :].astype(jnp.float32)
    return (forward, backward)


def body(embeddings, lengths):
    values = embeddings.astype(jnp.float32)
    unit = (values / jnp.sqrt(jnp.sum(values * values, axis=2, keepdims=True) + 1e-06)).astype(
        jnp.bfloat16
    )
    devices = lax.axis_size("sample")
    here = lax.axis_index("sample")
    per_dev = unit.shape[0]
    total = per_dev * devices
    base = here * per_dev
    piece = lax.all_gather(unit, "sample", axis=0, tiled=True)
    piece_len = lax.all_gather(lengths, "sample", axis=0, tiled=True)
    ahead, behind = tile_pairs(unit, lengths, piece, piece_len)
    own_index = base + jnp.arange(per_dev, dtype=jnp.int32)
    offdiag = jnp.arange(total, dtype=jnp.int32)[None, :] != own_index[:, None]
    utility = jnp.sum(jnp.where(offdiag, ahead + behind, jnp.float32(0.0)), axis=1)
    utility = utility / jnp.float32(2 * (total - 1))
    return (ahead, utility)


def solution(mesh):
    in_specs = (P(("prompt", "sample"), None, None), P(("prompt", "sample")))
    out_specs = (P(("prompt", "sample"), None), P(("prompt", "sample")))

    def run(embeddings, lengths):
        slots = mesh.shape["sample"]
        if mesh.shape["prompt"] == 4 and slots == 8 and embeddings.shape[0] == 1 and embeddings.shape[1] % (2 * T) == 0:
            return fused(slots, embeddings, lengths)
        return body(embeddings, lengths)

    return jax.shard_map(run, mesh=mesh, in_specs=in_specs, out_specs=out_specs, check_vma=False)
```

time: 52.9 us -> 59.9 us (1.13)
  Pallas kernels: 48.5 us -> 58.4 us
  between operations: 3.05 us -> 1.28 us
  local copies, waits for them, and re-layouts: 1.13 us -> 0 us
    pallas_call x1 -> x2, Pallas kernels: 48.5 us -> 58.4 us  [the longest x1 57.2 us: fused(): pl.pallas_call(functools.partial(kernel, slots // 2, slots), out_shape=ja...]
    unnamed x3 -> x0, local copies, waits for them, and re-layouts: 1.13 us -> none
where the time goes in v1:
time: 59.9 us; the launch traced here: 59.7 us
  Pallas kernels  58.4 us (97%)
  between operations  1.28 us (2%)
    pallas_call x1, Pallas kernels, fused(): pl.pallas_call(functools.partial(kernel, slots // 2, slots), out_shape=ja...  57.2 us

profile of v1, /device:TPU:0, one launch (start us, length us, event | category | flops | bytes accessed | tf_op | source)
XLA Modules:
  0.0 59.7 jit_solution(2581084152520844983)
XLA Ops:
  1.3 57.2 %shard_map.41.found_ref = f32[8,128]{1,0:T(8,128)} custom-call(bf16[1,512,1024]{2,1,0:T(8,128)(2,1)} %emb_ref.1, s32[1]{0:T(128)S(6)} %copy.4.len_ref), custom_call_target="tpu_custom_call" | custom-call | tf_op jit(solution)/shard_map/pallas_call | solution.py:420
  58.5 1.2 %shard_map.42 = (f32[1,8]{1,0:T(1,128)}, f32[1,1]{1,0:T(1,128)}) custom-call(f32[8,128]{1,0:T(8,128)} %shard_map.41.found_ref), custom_call_target="tpu_custom_call" | custom-call | tf_op jit(solution)/shard_map/pallas_call | solution.py:443

commit v2 on v1

--- a/solution.py
+++ b/solution.py
@@ -9,15 +9,20 @@
 
 MESH = pl.DeviceIdType.MESH
 T = 128
-FIRST = (32, 32, 64)
+PIECE = 64
+FIRST = (32, 32)
+FINAL = (32, 32)
+AHEAD = 2
+HOP = 2
+WINDOW = 128
 
 
 def pieces_of(length):
-    sizes = list(FIRST) + [T] * (length // T - sum(FIRST) // T)
+    sizes = list(FIRST) + [PIECE] * (length // PIECE - 2) + list(FINAL)
     return [(sum(sizes[:i]), n) for i, n in enumerate(sizes)]
 
 
-def kernel(chips, slots, emb_ref, len_ref, out_ref, stage, own, left, right, relay, count, lens, rows, cols, pair, res,
+def kernel(chips, slots, emb_ref, len_ref, out_ref, stage, own, left, right, relay, number, lens, rows, cols, pair, res,
            load, main_out, side_out, own_out, own_in, left_in, late_in, relay_in, relay_out, right_in, right_out,
            lens_out, lens_in, res_out, res_in):
     p, s = lax.axis_index("prompt"), lax.axis_index("sample")
@@ -29,6 +34,8 @@
     chunks = length // T
     halves = length // (2 * T)
     pieces = pieces_of(length)
+    count = length // PIECE
+    per = T // PIECE
     sib = 2 * z + 1 - c
     is_far, is_near, is_hub, is_end = v == 0, v == 1, v == 2, v == 3
     f32 = jnp.float32
@@ -85,27 +92,36 @@
     def fetch(k):
         return pltpu.make_async_copy(emb_ref.at[0, chunk(k)], stage.at[k], load.at[k])
 
-    fetch_len = pltpu.make_async_copy(len_ref, count, load.at[chunks])
+    fetch_len = pltpu.make_async_copy(len_ref, number, load.at[chunks])
     fetch_len.start()
     for k in range(chunks):
         fetch(k).start()
     fetch_len.wait()
-    mine = count[0]
+    mine = number[0]
     lens[s] = jnp.full(lens.shape[1:], mine, jnp.int32)
     token = lax.broadcasted_iota(jnp.int32, (T, 1), 0)
-    first = None
-    for k in range(chunks):
+
+    def scale(k, first):
         fetch(k).wait()
         values = stage[k].astype(f32)
         unit = values * (1.0 / jnp.sqrt(jnp.sum(values * values, axis=1, keepdims=True) + 1e-06))
         first = unit[0:1] if first is None else first
         own[0, k * T:(k + 1) * T] = jnp.where(token + k * T < mine, unit, first).astype(own.dtype)
-
-    def straight(k):
-        return copy(own.at[0, chunk(k)], left.at[k, 0], main_out.at[k], left_in.at[k], at(p, hub))
-
-    def inward(k):
-        return copy(own.at[0, chunk(k)], right.at[k, 0], main_out.at[k], right_in.at[0, k], at(p, hub))
+        return first
+
+    lead = scale(0, None)
+
+    def bit(m):
+        return pl.ds(m * PIECE, PIECE)
+
+    def spot(m):
+        return pl.ds(m % per * PIECE, PIECE)
+
+    def straight(m):
+        return copy(own.at[0, bit(m)], left.at[m // per, 0, spot(m)], main_out.at[m], left_in.at[m], at(p, hub))
+
+    def inward(m):
+        return copy(own.at[0, bit(m)], right.at[m // per, 0, spot(m)], main_out.at[m], right_in.at[0, m], at(p, hub))
 
     def detour(i):
         lo, n = pieces[i]
@@ -115,11 +131,12 @@
         lo, n = pieces[i]
         return copy(relay.at[pl.ds(lo, n)], left.at[lo // T, 1, pl.ds(lo % T, n)], relay_out.at[i], late_in.at[i], twin)
 
-    def outward(k, who):
-        return copy(own.at[0, chunk(k)], left.at[k, 0], side_out.at[k], left_in.at[k], at(p, who))
-
-    def to_side(k):
-        return copy(right.at[k, 0], right.at[k, 1], right_out.at[k], right_in.at[1, k], at(p, sib))
+    def outward(m, who):
+        return copy(own.at[0, bit(m)], left.at[m // per, 0, spot(m)], side_out.at[m], left_in.at[m], at(p, who))
+
+    def to_side(m):
+        return copy(right.at[m // per, 0, spot(m)], right.at[m // per, 1, spot(m)], right_out.at[m], right_in.at[1, m],
+                    at(p, sib))
 
     def tell(i, who):
         return copy(lens.at[s], lens.at[s], lens_out.at[i], lens_in.at[s], at(p, who))
@@ -132,50 +149,76 @@
 
     share = copy(own.at[0], own.at[1], own_out, own_in, at(p, sib))
 
+    def paced(send, lo, hi, ahead):
+        for i in range(lo, hi):
+            if i >= ahead:
+                send(i - ahead).wait_send()
+            send(i).start()
+
+    def turns(k):
+        if k == 0:
+            return [("in", 0), ("in", 1), ("on", 2), ("in", 2)]
+        m = per * k + 1
+        order = [("on", m), ("in", m), ("on", m + 1), ("on", m + 2), ("in", m + 1)]
+        done = [("on", m)] if k > 1 else []
+        return [turn for turn in order if turn[1] < count and turn not in done]
+
+    def before(i):
+        lo, n = pieces[i]
+        gone = [j for j, (start, size) in enumerate(pieces[:i]) if start < lo + n - WINDOW]
+        return max(gone) if gone else -1
+
+    def pass_on(m):
+        for i, (lo, n) in enumerate(pieces):
+            if lo // PIECE == m:
+                copy(relay.at[pl.ds(lo, n)], relay.at[pl.ds(lo, n)], relay_out.at[i], relay_in.at[i], twin).wait_recv()
+                freed = before(i)
+                for j in range(before(i - 1) + 1 if i else 0, freed + 1):
+                    hand_on(j).wait_send()
+                hand_on(i).start()
+
     @pl.when(is_far)
     def _():
         pl.semaphore_wait(barrier, 3)
-        for k in range(chunks):
-            straight(k).start()
         tell(1, hub).start()
+        paced(straight, 0, AHEAD, AHEAD)
 
     @pl.when(is_near)
     def _():
         pl.semaphore_wait(barrier, 4)
-        for i in range(len(pieces)):
-            detour(i).start()
-        for k in range(chunks):
-            outward(k, far).start()
+        paced(detour, 0, HOP, HOP)
         tell(1, hub).start()
         tell(2, far).start()
 
     @pl.when(is_hub)
     def _():
         pl.semaphore_wait(barrier, 6)
-        for k in range(chunks):
-            outward(k, end).start()
         tell(1, end).start()
 
     @pl.when(is_end)
     def _():
         pl.semaphore_wait(barrier, 3)
-        for k in range(chunks):
-            inward(k).start()
         tell(1, hub).start()
         tell(2, hub_other).start()
-
+        paced(inward, 0, AHEAD, AHEAD)
+
+    tell(0, sib).start()
+    for k in range(1, chunks):
+        scale(k, lead)
     share.start()
-    tell(0, sib).start()
-
-    def pass_on(i):
-        hand_wait = copy(relay.at[pl.ds(*pieces[i])], relay.at[pl.ds(*pieces[i])], relay_out.at[i], relay_in.at[i], twin)
-        hand_wait.wait_recv()
-        hand_on(i).start()
+
+    @pl.when(is_near)
+    def _():
+        for m in range(count):
+            outward(m, far).start()
+        paced(detour, HOP, len(pieces), HOP)
 
     @pl.when(is_hub)
     def _():
-        for i in range(len(FIRST) - 1):
-            pass_on(i)
+        for m in range(count):
+            outward(m, end).start()
+        pass_on(0)
+        pass_on(1)
 
     def dot(a, b):
         return lax.dot_general(a, b, (((1,), (1,)), ((), ())), preferred_element_type=f32)
@@ -293,7 +336,8 @@
         return b
 
     def arrived(k):
-        copy(left.at[k, 0], left.at[k, 0], main_out.at[k], left_in.at[k], at(p, hub)).wait_recv()
+        for m in range(per * k, per * k + per):
+            straight(m).wait_recv()
 
     @pl.when(is_hub)
     def _():
@@ -304,13 +348,14 @@
             if k == 0:
                 for who in ids + others:
                     told(who)
-                for i in range(len(FIRST) - 1, len(FIRST) + 1):
-                    pass_on(i)
-            elif len(FIRST) + k < len(pieces):
-                pass_on(len(FIRST) + k)
-            copy(right.at[k, 0], right.at[k, 0], right_out.at[k], right_in.at[0, k], at(p, sib)).wait_recv()
-            to_side(k).start()
-            to_side(k).wait_recv()
+            for kind, m in turns(k):
+                if kind == "on":
+                    pass_on(m)
+                else:
+                    inward(m).wait_recv()
+                    to_side(m).start()
+            for m in range(per * k, per * k + per):
+                to_side(m).wait_recv()
 
         def ready(k):
             arrived(k)
@@ -333,6 +378,14 @@
             if k == 0:
                 told(who)
 
+        @pl.when(is_far)
+        def _():
+            paced(straight, AHEAD, count, AHEAD)
+
+        @pl.when(is_end)
+        def _():
+            paced(inward, AHEAD, count, AHEAD)
+
         align([who], [], arrived, steps)
         report(0, 1, sib).start()
         report(1, 3, who).start()
@@ -344,10 +397,10 @@
     def _():
         res[0] = jnp.zeros(res.shape[1:], f32)
         res[1] = jnp.zeros(res.shape[1:], f32)
-        for i in range(len(pieces)):
+        for i in range(len(pieces) - HOP, len(pieces)):
             detour(i).wait_send()
-        for k in range(chunks):
-            outward(k, far).wait_send()
+        for m in range(count):
+            outward(m, far).wait_send()
         tell(1, hub).wait_send()
         tell(2, far).wait_send()
         reported(3)
@@ -356,8 +409,8 @@
     @pl.when(is_far)
     def _():
         res[3] = jnp.zeros(res.shape[1:], f32)
-        for k in range(chunks):
-            straight(k).wait_send()
+        for m in range(count - AHEAD, count):
+            straight(m).wait_send()
         tell(1, hub).wait_send()
         report(0, 1, sib).wait_send()
         report(1, 3, near).wait_send()
@@ -367,10 +420,10 @@
     @pl.when(is_hub)
     def _():
         res[2] = jnp.zeros(res.shape[1:], f32)
-        for k in range(chunks):
-            outward(k, end).wait_send()
-            to_side(k).wait_send()
-        for i in range(len(pieces)):
+        for m in range(count):
+            outward(m, end).wait_send()
+            to_side(m).wait_send()
+        for i in range(before(len(pieces) - 1) + 1, len(pieces)):
             hand_on(i).wait_send()
         tell(1, end).wait_send()
         reported(3)
@@ -378,8 +431,8 @@
 
     @pl.when(is_end)
     def _():
-        for k in range(chunks):
-            inward(k).wait_send()
+        for m in range(count - AHEAD, count):
+            inward(m).wait_send()
         tell(1, hub).wait_send()
         tell(2, hub_other).wait_send()
         report(0, 1, sib).wait_send()
@@ -414,13 +467,14 @@
     length, width = embeddings.shape[1:]
     chunks = length // T
     count = len(pieces_of(length))
+    many = length // PIECE
     dma = pltpu.SemaphoreType.DMA
     vmem = pl.BlockSpec(memory_space=pltpu.VMEM)
     away = pl.BlockSpec(memory_space=pl.ANY)
     found = pl.pallas_call(
         functools.partial(kernel, slots // 2, slots),
-        out_shape=jax.ShapeDtypeStruct((slots, T), jnp.float32),
-        in_specs=[away, away],
+        out_shape=pltpu.VMEM((slots, T), jnp.float32),
+        in_specs=[away, pl.BlockSpec(memory_space=pltpu.HBM)],
         out_specs=vmem,
         scratch_shapes=[
             pltpu.VMEM((chunks, T, width), jnp.bfloat16),
@@ -434,8 +488,8 @@
             pltpu.VMEM((chunks, 4, 8, 2 * T), jnp.float32),
             pltpu.VMEM((slots, T), jnp.float32),
             pltpu.VMEM((4, slots, T), jnp.float32),
-            dma((chunks + 1,)), dma((count,)), dma((chunks,)), dma(()), dma(()), dma((chunks,)), dma((count,)),
-            dma((count,)), dma((count,)), dma((2, chunks)), dma((chunks,)),
+            dma((chunks + 1,)), dma((count,)), dma((many,)), dma(()), dma(()), dma((many,)), dma((count,)),
+            dma((count,)), dma((count,)), dma((2, many)), dma((many,)),
             dma((3,)), dma((slots,)), dma((5,)), dma((4,)),
         ],
         compiler_params=pltpu.CompilerParams(collective_id=0, has_side_effects=True),
@@ -445,7 +499,7 @@
         out_shape=(jax.ShapeDtypeStruct((1, slots), jnp.float32), jax.ShapeDtypeStruct((1, 1), jnp.float32)),
         in_specs=[vmem],
         out_specs=(vmem, vmem),
-    )(found)
+    )(pltpu.with_memory_space_constraint(found, pltpu.VMEM))
     return precision, utility[:, 0]
 
 

time: 59.9 us -> 40 us (0.67)
  Pallas kernels: 58.4 us -> 38.5 us
    pallas_call x1, Pallas kernels: 57.2 us -> 38 us  [fused(): pl.pallas_call(functools.partial(kernel, slots // 2, slots), out_shape=pl...]
    pallas_call x1, Pallas kernels: 1.19 us -> 0.52 us  [fused(): pl.pallas_call(finish, out_shape=(jax.ShapeDtypeStruct((1, slots), jnp.fl...]
where the time goes in v2:
time: 40 us; the launch traced here: 39.8 us
  Pallas kernels  38.5 us (96%)
  between operations  1.28 us (3%)
    pallas_call x1, Pallas kernels, fused(): pl.pallas_call(functools.partial(kernel, slots // 2, slots), out_shape=pl...  38 us

profile of v2, /device:TPU:0, one launch (start us, length us, event | category | flops | bytes accessed | tf_op | source)
XLA Modules:
  0.0 39.8 jit_solution(15785997401327111178)
XLA Ops:
  1.3 38.0 %shard_map.41.found_ref = f32[8,128]{1,0:T(8,128)S(1)} custom-call(bf16[1,512,1024]{2,1,0:T(8,128)(2,1)} %emb_ref.1, s32[1]{0:T(128)S(6)} %copy.4.len_ref), custom_call_target="tpu_custom_call" | custom-call | tf_op jit(solution)/shard_map/pallas_call | solution.py:474
  39.3 0.5 %shard_map.42 = (f32[1,8]{1,0:T(1,128)}, f32[1,1]{1,0:T(1,128)}) custom-call(f32[8,128]{1,0:T(8,128)S(1)} %shard_map.41.found_ref), custom_call_target="tpu_custom_call" | custom-call | tf_op jit(solution)/shard_map/pallas_call | solution.py:497

commit v3 on v2

--- a/solution.py
+++ b/solution.py
@@ -11,19 +11,22 @@
 T = 128
 PIECE = 64
 FIRST = (32, 32)
-FINAL = (32, 32)
+FINAL = (16,)
+DIRECT = 48
 AHEAD = 2
 HOP = 2
 WINDOW = 128
+TURNS = 4
 
 
 def pieces_of(length):
-    sizes = list(FIRST) + [PIECE] * (length // PIECE - 2) + list(FINAL)
+    middle = length - sum(FIRST) - sum(FINAL) - DIRECT
+    sizes = list(FIRST) + [PIECE] * (middle // PIECE) + list(FINAL)
     return [(sum(sizes[:i]), n) for i, n in enumerate(sizes)]
 
 
 def kernel(chips, slots, emb_ref, len_ref, out_ref, stage, own, left, right, relay, number, lens, rows, cols, pair, res,
-           load, main_out, side_out, own_out, own_in, left_in, late_in, relay_in, relay_out, right_in, right_out,
+           load, main_out, side_out, own_out, own_in, left_in, late_in, relay_in, right_in, side_in, right_out,
            lens_out, lens_in, res_out, res_in):
     p, s = lax.axis_index("prompt"), lax.axis_index("sample")
     x, y, z, c = p % 2, p // 2, s // 2, s % 2
@@ -118,36 +121,47 @@
         return pl.ds(m % per * PIECE, PIECE)
 
     def straight(m):
-        return copy(own.at[0, bit(m)], left.at[m // per, 0, spot(m)], main_out.at[m], left_in.at[m], at(p, hub))
+        return copy(own.at[0, bit(m)], left.at[m // per, 0, spot(m)], main_out.at[m % AHEAD], left_in.at[m // per],
+                    at(p, hub))
 
     def inward(m):
-        return copy(own.at[0, bit(m)], right.at[m // per, 0, spot(m)], main_out.at[m], right_in.at[0, m], at(p, hub))
+        return copy(own.at[0, bit(m)], right.at[m // per, 0, spot(m)], main_out.at[m % AHEAD], right_in.at[m], at(p, hub))
 
     def detour(i):
         lo, n = pieces[i]
-        return copy(own.at[0, pl.ds(lo, n)], relay.at[pl.ds(lo, n)], main_out.at[i], relay_in.at[i], at(across, s))
+        return copy(own.at[0, pl.ds(lo, n)], relay.at[pl.ds(lo, n)], main_out.at[i % HOP], relay_in.at[i], at(across, s))
 
     def hand_on(i):
         lo, n = pieces[i]
-        return copy(relay.at[pl.ds(lo, n)], left.at[lo // T, 1, pl.ds(lo % T, n)], relay_out.at[i], late_in.at[i], twin)
-
-    def outward(m, who):
-        return copy(own.at[0, bit(m)], left.at[m // per, 0, spot(m)], side_out.at[m], left_in.at[m], at(p, who))
+        return copy(relay.at[pl.ds(lo, n)], left.at[lo // T, 1, pl.ds(lo % T, n)], main_out.at[i % TURNS],
+                    late_in.at[lo // T], twin)
+
+    shortcut = copy(own.at[0, pl.ds(length - DIRECT, DIRECT)], left.at[chunks - 1, 1, pl.ds(T - DIRECT, DIRECT)],
+                    own_out.at[1], late_in.at[chunks - 1], at(p, hub))
+
+    def outward(k, who):
+        return copy(own.at[0, chunk(k)], left.at[k, 0], side_out, left_in.at[k], at(p, who))
 
     def to_side(m):
-        return copy(right.at[m // per, 0, spot(m)], right.at[m // per, 1, spot(m)], right_out.at[m], right_in.at[1, m],
+        return copy(right.at[m // per, 0, spot(m)], right.at[m // per, 1, spot(m)], right_out, side_in.at[m // per],
                     at(p, sib))
 
     def tell(i, who):
-        return copy(lens.at[s], lens.at[s], lens_out.at[i], lens_in.at[s], at(p, who))
-
-    def told(who):
-        copy(lens.at[who], lens.at[who], lens_out.at[0], lens_in.at[who], at(p, sib)).wait_recv()
-
-    def report(i, slot, who):
-        return copy(res.at[0], res.at[slot], res_out.at[i], res_in.at[slot], at(p, who))
-
-    share = copy(own.at[0], own.at[1], own_out, own_in, at(p, sib))
+        return copy(lens.at[s], lens.at[s], lens_out, lens_in.at[i], at(p, who))
+
+    def told(i, who):
+        copy(lens.at[who], lens.at[who], lens_out, lens_in.at[i], at(p, sib)).wait_recv()
+
+    def all_sent(sem):
+        copy(own.at[0], own.at[0], sem, sem, at(p, sib)).wait_send()
+
+    def small_sent(sem, n):
+        copy(lens.at[pl.ds(0, n)], lens.at[pl.ds(0, n)], sem, sem, at(p, sib)).wait_send()
+
+    def report(slot, who):
+        return copy(res.at[0], res.at[slot], res_out, res_in.at[slot], at(p, who))
+
+    share = copy(own.at[0], own.at[1], own_out.at[0], own_in, at(p, sib))
 
     def paced(send, lo, hi, ahead):
         for i in range(lo, hi):
@@ -165,13 +179,13 @@
 
     def before(i):
         lo, n = pieces[i]
-        gone = [j for j, (start, size) in enumerate(pieces[:i]) if start < lo + n - WINDOW]
+        gone = [j for j, (start, size) in enumerate(pieces[:i]) if start < lo + n - WINDOW or j <= i - TURNS]
         return max(gone) if gone else -1
 
     def pass_on(m):
         for i, (lo, n) in enumerate(pieces):
             if lo // PIECE == m:
-                copy(relay.at[pl.ds(lo, n)], relay.at[pl.ds(lo, n)], relay_out.at[i], relay_in.at[i], twin).wait_recv()
+                copy(relay.at[pl.ds(lo, n)], relay.at[pl.ds(lo, n)], main_out.at[0], relay_in.at[i], twin).wait_recv()
                 freed = before(i)
                 for j in range(before(i - 1) + 1 if i else 0, freed + 1):
                     hand_on(j).wait_send()
@@ -187,8 +201,8 @@
     def _():
         pl.semaphore_wait(barrier, 4)
         paced(detour, 0, HOP, HOP)
-        tell(1, hub).start()
-        tell(2, far).start()
+        tell(2, hub).start()
+        tell(1, far).start()
 
     @pl.when(is_hub)
     def _():
@@ -198,8 +212,8 @@
     @pl.when(is_end)
     def _():
         pl.semaphore_wait(barrier, 3)
-        tell(1, hub).start()
-        tell(2, hub_other).start()
+        tell(3, hub).start()
+        tell(4, hub_other).start()
         paced(inward, 0, AHEAD, AHEAD)
 
     tell(0, sib).start()
@@ -209,14 +223,15 @@
 
     @pl.when(is_near)
     def _():
-        for m in range(count):
-            outward(m, far).start()
+        for k in range(chunks):
+            outward(k, far).start()
         paced(detour, HOP, len(pieces), HOP)
+        shortcut.start()
 
     @pl.when(is_hub)
     def _():
-        for m in range(count):
-            outward(m, end).start()
+        for k in range(chunks):
+            outward(k, end).start()
         pass_on(0)
         pass_on(1)
 
@@ -256,7 +271,7 @@
 
     ours = [s, sib]
     share.wait_recv()
-    told(sib)
+    told(0, sib)
     by_row = [None] * halves
     by_col = [None, None]
     for h in range(halves):
@@ -336,8 +351,7 @@
         return b
 
     def arrived(k):
-        for m in range(per * k, per * k + per):
-            straight(m).wait_recv()
+        copy(left.at[k, 0], left.at[k, 0], side_out, left_in.at[k], at(p, sib)).wait_recv()
 
     @pl.when(is_hub)
     def _():
@@ -346,29 +360,26 @@
 
         def steps(k):
             if k == 0:
-                for who in ids + others:
-                    told(who)
+                for i, who in enumerate(ids + others):
+                    told(1 + i, who)
             for kind, m in turns(k):
                 if kind == "on":
                     pass_on(m)
                 else:
                     inward(m).wait_recv()
                     to_side(m).start()
-            for m in range(per * k, per * k + per):
-                to_side(m).wait_recv()
+            copy(right.at[k, 1], right.at[k, 1], right_out, side_in.at[k], at(p, sib)).wait_recv()
 
         def ready(k):
             arrived(k)
-            for i, (lo, n) in enumerate(pieces):
-                if lo // T == k:
-                    hand_on(i).wait_recv()
+            copy(left.at[k, 1], left.at[k, 1], side_out, late_in.at[k], at(p, sib)).wait_recv()
 
         align(ids, others, ready, steps)
-        report(0, 1, sib).start()
-        report(1, 2, far).start()
-        report(2, 2, near).start()
-        report(3, 2, end).start()
-        report(4, 3, end_other).start()
+        report(1, sib).start()
+        report(2, far).start()
+        report(2, near).start()
+        report(2, end).start()
+        report(3, end_other).start()
 
     @pl.when(is_far | is_end)
     def _():
@@ -376,7 +387,7 @@
 
         def steps(k):
             if k == 0:
-                told(who)
+                told(1, who)
 
         @pl.when(is_far)
         def _():
@@ -387,11 +398,11 @@
             paced(inward, AHEAD, count, AHEAD)
 
         align([who], [], arrived, steps)
-        report(0, 1, sib).start()
-        report(1, 3, who).start()
+        report(1, sib).start()
+        report(3, who).start()
 
     def reported(slot):
-        copy(res.at[slot], res.at[slot], res_out.at[0], res_in.at[slot], at(p, sib)).wait_recv()
+        copy(res.at[slot], res.at[slot], res_out, res_in.at[slot], at(p, sib)).wait_recv()
 
     @pl.when(is_near)
     def _():
@@ -399,10 +410,9 @@
         res[1] = jnp.zeros(res.shape[1:], f32)
         for i in range(len(pieces) - HOP, len(pieces)):
             detour(i).wait_send()
-        for m in range(count):
-            outward(m, far).wait_send()
-        tell(1, hub).wait_send()
-        tell(2, far).wait_send()
+        shortcut.wait_send()
+        all_sent(side_out)
+        small_sent(lens_out, 3)
         reported(3)
         reported(2)
 
@@ -411,21 +421,19 @@
         res[3] = jnp.zeros(res.shape[1:], f32)
         for m in range(count - AHEAD, count):
             straight(m).wait_send()
-        tell(1, hub).wait_send()
-        report(0, 1, sib).wait_send()
-        report(1, 3, near).wait_send()
+        small_sent(lens_out, 2)
+        small_sent(res_out, 2)
         reported(1)
         reported(2)
 
     @pl.when(is_hub)
     def _():
         res[2] = jnp.zeros(res.shape[1:], f32)
-        for m in range(count):
-            outward(m, end).wait_send()
-            to_side(m).wait_send()
+        all_sent(side_out)
+        all_sent(right_out)
         for i in range(before(len(pieces) - 1) + 1, len(pieces)):
             hand_on(i).wait_send()
-        tell(1, end).wait_send()
+        small_sent(lens_out, 2)
         reported(3)
         reported(1)
 
@@ -433,10 +441,8 @@
     def _():
         for m in range(count - AHEAD, count):
             inward(m).wait_send()
-        tell(1, hub).wait_send()
-        tell(2, hub_other).wait_send()
-        report(0, 1, sib).wait_send()
-        report(1, 3, hub).wait_send()
+        small_sent(lens_out, 3)
+        small_sent(res_out, 2)
         for slot in range(1, 4):
             reported(slot)
 
@@ -447,15 +453,10 @@
     score = jnp.sum(both, axis=1, keepdims=True) / f32(2 * (slots - 1))
     out_ref[...] = jnp.where(high == 0, row, score)
     share.wait_send()
-    tell(0, sib).wait_send()
 
     @pl.when(is_hub)
     def _():
-        report(0, 1, sib).wait_send()
-        report(1, 2, far).wait_send()
-        report(2, 2, near).wait_send()
-        report(3, 2, end).wait_send()
-        report(4, 3, end_other).wait_send()
+        small_sent(res_out, 5)
 
 
 def finish(found_ref, precision_ref, utility_ref):
@@ -488,9 +489,9 @@
             pltpu.VMEM((chunks, 4, 8, 2 * T), jnp.float32),
             pltpu.VMEM((slots, T), jnp.float32),
             pltpu.VMEM((4, slots, T), jnp.float32),
-            dma((chunks + 1,)), dma((count,)), dma((many,)), dma(()), dma(()), dma((many,)), dma((count,)),
-            dma((count,)), dma((count,)), dma((2, many)), dma((many,)),
-            dma((3,)), dma((slots,)), dma((5,)), dma((4,)),
+            dma((chunks + 1,)), dma((max(AHEAD, HOP, TURNS),)), dma(()), dma((2,)), dma(()), dma((chunks,)),
+            dma((chunks,)), dma((count,)), dma((many,)), dma((chunks,)), dma(()),
+            dma(()), dma((5,)), dma(()), dma((4,)),
         ],
         compiler_params=pltpu.CompilerParams(collective_id=0, has_side_effects=True),
     )(embeddings, lengths)

time: 40 us -> 37.8 us (0.945)
  Pallas kernels: 38.5 us -> 36.4 us
    pallas_call x1, Pallas kernels: 38 us -> 35.9 us  [fused(): pl.pallas_call(functools.partial(kernel, slots // 2, slots), out_shape=pl...]
where the time goes in v3:
time: 37.8 us; the launch traced here: 37.7 us
  Pallas kernels  36.4 us (96%)
  between operations  1.28 us (3%)
    pallas_call x1, Pallas kernels, fused(): pl.pallas_call(functools.partial(kernel, slots // 2, slots), out_shape=pl...  35.9 us

profile of v3, /device:TPU:0, one launch (start us, length us, event | category | flops | bytes accessed | tf_op | source)
XLA Modules:
  0.0 37.7 jit_solution(14447289235792742157)
XLA Ops:
  1.3 35.9 %shard_map.41.found_ref = f32[8,128]{1,0:T(8,128)S(1)} custom-call(bf16[1,512,1024]{2,1,0:T(8,128)(2,1)} %emb_ref.1, s32[1]{0:T(128)S(6)} %copy.4.len_ref), custom_call_target="tpu_custom_call" | custom-call | tf_op jit(solution)/shard_map/pallas_call | solution.py:475
  37.1 0.5 %shard_map.42 = (f32[1,8]{1,0:T(1,128)}, f32[1,1]{1,0:T(1,128)}) custom-call(f32[8,128]{1,0:T(8,128)S(1)} %shard_map.41.found_ref), custom_call_target="tpu_custom_call" | custom-call | tf_op jit(solution)/shard_map/pallas_call | solution.py:498

commit v4 on v3

--- a/solution.py
+++ b/solution.py
@@ -10,18 +10,18 @@
 MESH = pl.DeviceIdType.MESH
 T = 128
 PIECE = 64
-FIRST = (32, 32)
-FINAL = (16,)
-DIRECT = 48
+FIRST = (16, 16, 32)
+DIRECT = (32, 48)
 AHEAD = 2
-HOP = 2
-WINDOW = 128
+HOP = 3
+WINDOW = 192
 TURNS = 4
 
 
-def pieces_of(length):
-    middle = length - sum(FIRST) - sum(FINAL) - DIRECT
-    sizes = list(FIRST) + [PIECE] * (middle // PIECE) + list(FINAL)
+def pieces_of(length, direct):
+    sizes = list(FIRST)
+    while sum(sizes) < length - direct:
+        sizes.append(min(PIECE, length - direct - sum(sizes)))
     return [(sum(sizes[:i]), n) for i, n in enumerate(sizes)]
 
 
@@ -36,7 +36,7 @@
     length, width = own.shape[1:]
     chunks = length // T
     halves = length // (2 * T)
-    pieces = pieces_of(length)
+    plans = [pieces_of(length, direct) for direct in DIRECT]
     count = length // PIECE
     per = T // PIECE
     sib = 2 * z + 1 - c
@@ -127,17 +127,23 @@
     def inward(m):
         return copy(own.at[0, bit(m)], right.at[m // per, 0, spot(m)], main_out.at[m % AHEAD], right_in.at[m], at(p, hub))
 
-    def detour(i):
-        lo, n = pieces[i]
+    def detour(f, i):
+        lo, n = plans[f][i]
         return copy(own.at[0, pl.ds(lo, n)], relay.at[pl.ds(lo, n)], main_out.at[i % HOP], relay_in.at[i], at(across, s))
 
-    def hand_on(i):
-        lo, n = pieces[i]
+    def hand_on(f, i):
+        lo, n = plans[f][i]
         return copy(relay.at[pl.ds(lo, n)], left.at[lo // T, 1, pl.ds(lo % T, n)], main_out.at[i % TURNS],
                     late_in.at[lo // T], twin)
 
-    shortcut = copy(own.at[0, pl.ds(length - DIRECT, DIRECT)], left.at[chunks - 1, 1, pl.ds(T - DIRECT, DIRECT)],
+    def shortcut(f):
+        n = DIRECT[f]
+        return copy(own.at[0, pl.ds(length - n, n)], left.at[chunks - 1, 1, pl.ds(T - n, n)],
                     own_out.at[1], late_in.at[chunks - 1], at(p, hub))
+
+    def by_line(which, do):
+        for f in range(2):
+            pl.when(which == f)(functools.partial(do, f))
 
     def outward(k, who):
         return copy(own.at[0, chunk(k)], left.at[k, 0], side_out, left_in.at[k], at(p, who))
@@ -170,26 +176,43 @@
             send(i).start()
 
     def turns(k):
-        if k == 0:
-            return [("in", 0), ("in", 1), ("on", 2), ("in", 2)]
-        m = per * k + 1
-        order = [("on", m), ("in", m), ("on", m + 1), ("on", m + 2), ("in", m + 1)]
-        done = [("on", m)] if k > 1 else []
-        return [turn for turn in order if turn[1] < count and turn not in done]
-
-    def before(i):
-        lo, n = pieces[i]
-        gone = [j for j, (start, size) in enumerate(pieces[:i]) if start < lo + n - WINDOW or j <= i - TURNS]
+        return {
+            0: [("in", 0), ("in", 1), ("on", 2), ("in", 2), ("on", 3)],
+            1: [("in", 3), ("on", 4), ("in", 4), ("on", 5), ("in", 5), ("on", 6)],
+            2: [("on", 7), ("in", 6)]}.get(k, [])
+
+    def late_turns(k):
+        return {2: [("in", 7)]}.get(k, [])
+
+    def before(f, i):
+        lo, n = plans[f][i]
+        gone = [j for j, (start, size) in enumerate(plans[f][:i]) if start < lo + n - WINDOW or j <= i - TURNS]
         return max(gone) if gone else -1
 
     def pass_on(m):
-        for i, (lo, n) in enumerate(pieces):
-            if lo // PIECE == m:
-                copy(relay.at[pl.ds(lo, n)], relay.at[pl.ds(lo, n)], main_out.at[0], relay_in.at[i], twin).wait_recv()
-                freed = before(i)
-                for j in range(before(i - 1) + 1 if i else 0, freed + 1):
-                    hand_on(j).wait_send()
-                hand_on(i).start()
+        def do(f):
+            for i, (lo, n) in enumerate(plans[f]):
+                if lo // PIECE == m:
+                    part = relay.at[pl.ds(lo, n)]
+                    copy(part, part, main_out.at[0], relay_in.at[i], twin).wait_recv()
+                    for j in range(before(f, i - 1) + 1 if i else 0, before(f, i) + 1):
+                        hand_on(f, j).wait_send()
+                    hand_on(f, i).start()
+
+        by_line(1 - flip, do)
+
+    def passed_on(f):
+        for i in range(before(f, len(plans[f]) - 1) + 1, len(plans[f])):
+            hand_on(f, i).wait_send()
+
+    def detour_rest(f):
+        paced(functools.partial(detour, f), HOP, len(plans[f]), HOP)
+        shortcut(f).start()
+
+    def detour_sent(f):
+        for i in range(len(plans[f]) - HOP, len(plans[f])):
+            detour(f, i).wait_send()
+        shortcut(f).wait_send()
 
     @pl.when(is_far)
     def _():
@@ -200,7 +223,7 @@
     @pl.when(is_near)
     def _():
         pl.semaphore_wait(barrier, 4)
-        paced(detour, 0, HOP, HOP)
+        paced(functools.partial(detour, 0), 0, HOP, HOP)
         tell(2, hub).start()
         tell(1, far).start()
 
@@ -225,8 +248,7 @@
     def _():
         for k in range(chunks):
             outward(k, far).start()
-        paced(detour, HOP, len(pieces), HOP)
-        shortcut.start()
+        by_line(flip, detour_rest)
 
     @pl.when(is_hub)
     def _():
@@ -293,7 +315,7 @@
         total = plus(total, row_sum(by_row[g], 2 * T * g, sib))
     pair[...] = put(table, sib, s, total)
 
-    def align(ids, others, ready, steps):
+    def align(ids, others, ready, steps, halfway=None):
         n = len(ids)
         sums = {}
         for k in range(chunks):
@@ -328,6 +350,7 @@
                     best[b] = fold(best[b], down(part))
                     meet(part, b * halves + h, k == 0, [(0, 2 * T, 2 * T * h, ours[b], ours_key(b))])
             if others:
+                halfway(k)
                 for j in range(k + 1):
                     part = dot(right[j].reshape(2 * T, width), y_side)
                     for b in range(2):
@@ -336,15 +359,24 @@
                          [(b * T, T, j * T, others[b], 2 + b) for b in range(2)])
             for b in range(4 if others else 2):
                 cols[k, b, :, :n * T] = best[b]
+        whose = ours + list(others)
         table = jnp.zeros((slots, T), f32)
-        whose = ours + list(others)
         for b in range(len(whose)):
+            spread = jnp.zeros((8, T), f32)
             for a in range(n):
+                spread = jnp.where(wide == ids[a], sums[b, a], spread)
+            line = jnp.sum(spread, axis=0, keepdims=True) / length_of(whose[b]).astype(f32)
+            table = jnp.where(high == whose[b], line, table)
+        for a in range(n):
+            stack = jnp.zeros((slots, T), f32)
+            for b in range(len(whose)):
                 across_sum = None
                 for k in range(chunks):
                     across_sum = plus(across_sum, col_sum(cols[k, b, :, a * T:(a + 1) * T], k * T, ids[a]))
-                table = put(table, ids[a], whose[b], across_sum)
-                table = put(table, whose[b], ids[a], sums[b, a])
+                stack = jnp.where(high == whose[b], across_sum, stack)
+            totals = jnp.where(high == wide, jnp.sum(stack, axis=1, keepdims=True), f32(0.0))
+            line = jnp.sum(totals, axis=0, keepdims=True) / length_of(ids[a]).astype(f32)
+            table = jnp.where(high == ids[a], line, table)
         res[0] = table
 
     def ours_key(b):
@@ -358,28 +390,34 @@
         ids = [far, near]
         others = [end, end_other]
 
-        def steps(k):
-            if k == 0:
-                for i, who in enumerate(ids + others):
-                    told(1 + i, who)
-            for kind, m in turns(k):
+        def take(turns):
+            for kind, m in turns:
                 if kind == "on":
                     pass_on(m)
                 else:
                     inward(m).wait_recv()
                     to_side(m).start()
+
+        def halfway(k):
+            take(late_turns(k))
+
+        def steps(k):
+            if k == 0:
+                for i, who in enumerate(ids + others):
+                    told(1 + i, who)
+            take(turns(k))
             copy(right.at[k, 1], right.at[k, 1], right_out, side_in.at[k], at(p, sib)).wait_recv()
 
         def ready(k):
             arrived(k)
             copy(left.at[k, 1], left.at[k, 1], side_out, late_in.at[k], at(p, sib)).wait_recv()
 
-        align(ids, others, ready, steps)
-        report(1, sib).start()
+        align(ids, others, ready, steps, halfway)
         report(2, far).start()
         report(2, near).start()
         report(2, end).start()
         report(3, end_other).start()
+        report(1, sib).start()
 
     @pl.when(is_far | is_end)
     def _():
@@ -408,9 +446,7 @@
     def _():
         res[0] = jnp.zeros(res.shape[1:], f32)
         res[1] = jnp.zeros(res.shape[1:], f32)
-        for i in range(len(pieces) - HOP, len(pieces)):
-            detour(i).wait_send()
-        shortcut.wait_send()
+        by_line(flip, detour_sent)
         all_sent(side_out)
         small_sent(lens_out, 3)
         reported(3)
@@ -431,8 +467,7 @@
         res[2] = jnp.zeros(res.shape[1:], f32)
         all_sent(side_out)
         all_sent(right_out)
-        for i in range(before(len(pieces) - 1) + 1, len(pieces)):
-            hand_on(i).wait_send()
+        by_line(1 - flip, passed_on)
         small_sent(lens_out, 2)
         reported(3)
         reported(1)
@@ -467,7 +502,7 @@
 def fused(slots, embeddings, lengths):
     length, width = embeddings.shape[1:]
     chunks = length // T
-    count = len(pieces_of(length))
+    count = max(len(pieces_of(length, direct)) for direct in DIRECT)
     many = length // PIECE
     dma = pltpu.SemaphoreType.DMA
     vmem = pl.BlockSpec(memory_space=pltpu.VMEM)
@@ -546,7 +581,7 @@
 
     def run(embeddings, lengths):
         slots = mesh.shape["sample"]
-        if mesh.shape["prompt"] == 4 and slots == 8 and embeddings.shape[0] == 1 and embeddings.shape[1] % (2 * T) == 0:
+        if mesh.shape["prompt"] == 4 and slots == 8 and embeddings.shape[0] == 1 and embeddings.shape[1] == 4 * T:
             return fused(slots, embeddings, lengths)
         return body(embeddings, lengths)
 

time: 37.8 us -> 37.4 us (0.989)
  Pallas kernels: 36.4 us -> 36 us
    pallas_call x1, Pallas kernels: 35.9 us -> 35.4 us  [fused(): pl.pallas_call(functools.partial(kernel, slots // 2, slots), out_shape=pl...]
where the time goes in v4:
time: 37.4 us; the launch traced here: 37.2 us
  Pallas kernels  36 us (96%)
  between operations  1.28 us (3%)
    pallas_call x1, Pallas kernels, fused(): pl.pallas_call(functools.partial(kernel, slots // 2, slots), out_shape=pl...  35.4 us

profile of v4, /device:TPU:0, one launch (start us, length us, event | category | flops | bytes accessed | tf_op | source)
XLA Modules:
  0.0 37.2 jit_solution(10964381975624529822)
XLA Ops:
  1.3 35.4 %shard_map.41.found_ref = f32[8,128]{1,0:T(8,128)S(1)} custom-call(bf16[1,512,1024]{2,1,0:T(8,128)(2,1)} %emb_ref.1, s32[1]{0:T(128)S(6)} %copy.4.len_ref), custom_call_target="tpu_custom_call" | custom-call | tf_op jit(solution)/shard_map/pallas_call | solution.py:510
  36.7 0.5 %shard_map.42 = (f32[1,8]{1,0:T(1,128)}, f32[1,1]{1,0:T(1,128)}) custom-call(f32[8,128]{1,0:T(8,128)S(1)} %shard_map.41.found_ref), custom_call_target="tpu_custom_call" | custom-call | tf_op jit(solution)/shard_map/pallas_call | solution.py:533

commit v5 on v4

--- a/solution.py
+++ b/solution.py
@@ -11,10 +11,11 @@
 T = 128
 PIECE = 64
 FIRST = (16, 16, 32)
-DIRECT = (32, 48)
+DIRECT = (32, 48, 48, 48)
 AHEAD = 2
-HOP = 3
-WINDOW = 192
+MORE = 3
+HOP = (3, 3, 3, 3)
+WINDOW = (256, 192, 192, 128)
 TURNS = 4
 
 
@@ -121,15 +122,15 @@
         return pl.ds(m % per * PIECE, PIECE)
 
     def straight(m):
-        return copy(own.at[0, bit(m)], left.at[m // per, 0, spot(m)], main_out.at[m % AHEAD], left_in.at[m // per],
+        return copy(own.at[0, bit(m)], left.at[m // per, 0, spot(m)], main_out.at[m % TURNS], left_in.at[m // per],
                     at(p, hub))
 
     def inward(m):
-        return copy(own.at[0, bit(m)], right.at[m // per, 0, spot(m)], main_out.at[m % AHEAD], right_in.at[m], at(p, hub))
+        return copy(own.at[0, bit(m)], right.at[m // per, 0, spot(m)], main_out.at[m % TURNS], right_in.at[m], at(p, hub))
 
     def detour(f, i):
         lo, n = plans[f][i]
-        return copy(own.at[0, pl.ds(lo, n)], relay.at[pl.ds(lo, n)], main_out.at[i % HOP], relay_in.at[i], at(across, s))
+        return copy(own.at[0, pl.ds(lo, n)], relay.at[pl.ds(lo, n)], main_out.at[i % TURNS], relay_in.at[i], at(across, s))
 
     def hand_on(f, i):
         lo, n = plans[f][i]
@@ -142,7 +143,7 @@
                     own_out.at[1], late_in.at[chunks - 1], at(p, hub))
 
     def by_line(which, do):
-        for f in range(2):
+        for f in range(len(DIRECT)):
             pl.when(which == f)(functools.partial(do, f))
 
     def outward(k, who):
@@ -179,14 +180,12 @@
         return {
             0: [("in", 0), ("in", 1), ("on", 2), ("in", 2), ("on", 3)],
             1: [("in", 3), ("on", 4), ("in", 4), ("on", 5), ("in", 5), ("on", 6)],
-            2: [("on", 7), ("in", 6)]}.get(k, [])
-
-    def late_turns(k):
-        return {2: [("in", 7)]}.get(k, [])
+            2: [("on", 7), ("in", 6)],
+            3: [("in", 7)]}[k]
 
     def before(f, i):
         lo, n = plans[f][i]
-        gone = [j for j, (start, size) in enumerate(plans[f][:i]) if start < lo + n - WINDOW or j <= i - TURNS]
+        gone = [j for j, (start, size) in enumerate(plans[f][:i]) if start < lo + n - WINDOW[f] or j <= i - TURNS]
         return max(gone) if gone else -1
 
     def pass_on(m):
@@ -199,20 +198,31 @@
                         hand_on(f, j).wait_send()
                     hand_on(f, i).start()
 
-        by_line(1 - flip, do)
+        by_line(across, do)
 
     def passed_on(f):
         for i in range(before(f, len(plans[f]) - 1) + 1, len(plans[f])):
             hand_on(f, i).wait_send()
 
     def detour_rest(f):
-        paced(functools.partial(detour, f), HOP, len(plans[f]), HOP)
+        paced(functools.partial(detour, f), min(HOP), len(plans[f]), HOP[f])
         shortcut(f).start()
 
     def detour_sent(f):
-        for i in range(len(plans[f]) - HOP, len(plans[f])):
+        for i in range(len(plans[f]) - HOP[f], len(plans[f])):
             detour(f, i).wait_send()
         shortcut(f).wait_send()
+
+    def done(send, window):
+        for m in range(count - window, count):
+            send(m).wait_send()
+
+    def by_window(wider, do):
+        pl.when(wider)(lambda: do(MORE))
+        pl.when(jnp.logical_not(wider))(lambda: do(AHEAD))
+
+    ahead_of = (p == 0) & (c == 0)
+    behind = (p == 0) & (c == 1)
 
     @pl.when(is_far)
     def _():
@@ -223,7 +233,7 @@
     @pl.when(is_near)
     def _():
         pl.semaphore_wait(barrier, 4)
-        paced(functools.partial(detour, 0), 0, HOP, HOP)
+        paced(functools.partial(detour, 0), 0, min(HOP), min(HOP))
         tell(2, hub).start()
         tell(1, far).start()
 
@@ -248,7 +258,7 @@
     def _():
         for k in range(chunks):
             outward(k, far).start()
-        by_line(flip, detour_rest)
+        by_line(p, detour_rest)
 
     @pl.when(is_hub)
     def _():
@@ -315,7 +325,7 @@
         total = plus(total, row_sum(by_row[g], 2 * T * g, sib))
     pair[...] = put(table, sib, s, total)
 
-    def align(ids, others, ready, steps, halfway=None):
+    def align(ids, others, ready, steps, landed=None):
         n = len(ids)
         sums = {}
         for k in range(chunks):
@@ -333,7 +343,8 @@
                         add = row_sum(best[lo:lo + size], start, who)
                         sums[key, a] = plus(sums.get((key, a)), add)
 
-            if others:
+            def catch_up():
+                landed(k)
                 x_side = right[k].reshape(2 * T, width)
                 r = 2 * halves + k
                 for j in range(k):
@@ -341,6 +352,9 @@
                     for b in range(2):
                         cols[j, 2 + b] = jnp.maximum(cols[j, 2 + b], down(part[b * T:(b + 1) * T]))
                     rows[r] = part if j == 0 else jnp.maximum(rows[r], part)
+
+            if others:
+                catch_up()
             ready(k)
             y_side = left[k, :n].reshape(n * T, width)
             best = [None] * 4
@@ -350,7 +364,6 @@
                     best[b] = fold(best[b], down(part))
                     meet(part, b * halves + h, k == 0, [(0, 2 * T, 2 * T * h, ours[b], ours_key(b))])
             if others:
-                halfway(k)
                 for j in range(k + 1):
                     part = dot(right[j].reshape(2 * T, width), y_side)
                     for b in range(2):
@@ -398,21 +411,20 @@
                     inward(m).wait_recv()
                     to_side(m).start()
 
-        def halfway(k):
-            take(late_turns(k))
-
         def steps(k):
             if k == 0:
                 for i, who in enumerate(ids + others):
                     told(1 + i, who)
             take(turns(k))
+
+        def landed(k):
             copy(right.at[k, 1], right.at[k, 1], right_out, side_in.at[k], at(p, sib)).wait_recv()
 
         def ready(k):
             arrived(k)
             copy(left.at[k, 1], left.at[k, 1], side_out, late_in.at[k], at(p, sib)).wait_recv()
 
-        align(ids, others, ready, steps, halfway)
+        align(ids, others, ready, steps, landed)
         report(2, far).start()
         report(2, near).start()
         report(2, end).start()
@@ -429,11 +441,11 @@
 
         @pl.when(is_far)
         def _():
-            paced(straight, AHEAD, count, AHEAD)
+            by_window(ahead_of, lambda window: paced(straight, AHEAD, count, window))
 
         @pl.when(is_end)
         def _():
-            paced(inward, AHEAD, count, AHEAD)
+            by_window(behind, lambda window: paced(inward, AHEAD, count, window))
 
         align([who], [], arrived, steps)
         report(1, sib).start()
@@ -446,7 +458,7 @@
     def _():
         res[0] = jnp.zeros(res.shape[1:], f32)
         res[1] = jnp.zeros(res.shape[1:], f32)
-        by_line(flip, detour_sent)
+        by_line(p, detour_sent)
         all_sent(side_out)
         small_sent(lens_out, 3)
         reported(3)
@@ -455,8 +467,7 @@
     @pl.when(is_far)
     def _():
         res[3] = jnp.zeros(res.shape[1:], f32)
-        for m in range(count - AHEAD, count):
-            straight(m).wait_send()
+        by_window(ahead_of, lambda window: done(straight, window))
         small_sent(lens_out, 2)
         small_sent(res_out, 2)
         reported(1)
@@ -467,15 +478,14 @@
         res[2] = jnp.zeros(res.shape[1:], f32)
         all_sent(side_out)
         all_sent(right_out)
-        by_line(1 - flip, passed_on)
+        by_line(across, passed_on)
         small_sent(lens_out, 2)
         reported(3)
         reported(1)
 
     @pl.when(is_end)
     def _():
-        for m in range(count - AHEAD, count):
-            inward(m).wait_send()
+        by_window(behind, lambda window: done(inward, window))
         small_sent(lens_out, 3)
         small_sent(res_out, 2)
         for slot in range(1, 4):
@@ -524,7 +534,7 @@
             pltpu.VMEM((chunks, 4, 8, 2 * T), jnp.float32),
             pltpu.VMEM((slots, T), jnp.float32),
             pltpu.VMEM((4, slots, T), jnp.float32),
-            dma((chunks + 1,)), dma((max(AHEAD, HOP, TURNS),)), dma(()), dma((2,)), dma(()), dma((chunks,)),
+            dma((chunks + 1,)), dma((TURNS,)), dma(()), dma((2,)), dma(()), dma((chunks,)),
             dma((chunks,)), dma((count,)), dma((many,)), dma((chunks,)), dma(()),
             dma(()), dma((5,)), dma(()), dma((4,)),
         ],

time: 37.4 us -> 37.1 us (level)
  no operation moved by 1% of the time
where the time goes in v5:
time: 37.1 us; the launch traced here: 37 us
  Pallas kernels  35.7 us (96%)
  between operations  1.28 us (3%)
    pallas_call x1, Pallas kernels, fused(): pl.pallas_call(functools.partial(kernel, slots // 2, slots), out_shape=pl...  35.2 us

profile of v5, /device:TPU:0, one launch (start us, length us, event | category | flops | bytes accessed | tf_op | source)
XLA Modules:
  0.0 37.0 jit_solution(1304570594783514308)
XLA Ops:
  1.3 35.2 %shard_map.41.found_ref = f32[8,128]{1,0:T(8,128)S(1)} custom-call(bf16[1,512,1024]{2,1,0:T(8,128)(2,1)} %emb_ref.1, s32[1]{0:T(128)S(6)} %copy.4.len_ref), custom_call_target="tpu_custom_call" | custom-call | tf_op jit(solution)/shard_map/pallas_call | solution.py:520
  36.5 0.5 %shard_map.42 = (f32[1,8]{1,0:T(1,128)}, f32[1,1]{1,0:T(1,128)}) custom-call(f32[8,128]{1,0:T(8,128)S(1)} %shard_map.41.found_ref), custom_call_target="tpu_custom_call" | custom-call | tf_op jit(solution)/shard_map/pallas_call | solution.py:543

commit v6 on v5

--- a/solution.py
+++ b/solution.py
@@ -11,10 +11,10 @@
 T = 128
 PIECE = 64
 FIRST = (16, 16, 32)
-DIRECT = (32, 48, 48, 48)
+DIRECT = (16, 48, 48, 64)
 AHEAD = 2
-MORE = 3
-HOP = (3, 3, 3, 3)
+MORE = 4
+HOP = (4, 3, 3, 2)
 WINDOW = (256, 192, 192, 128)
 TURNS = 4
 
@@ -94,11 +94,12 @@
         greet(at(p, hub_other))
 
     def fetch(k):
-        return pltpu.make_async_copy(emb_ref.at[0, chunk(k)], stage.at[k], load.at[k])
-
-    fetch_len = pltpu.make_async_copy(len_ref, number, load.at[chunks])
+        n = 1 if k == 0 else chunks - 1
+        return pltpu.make_async_copy(emb_ref.at[0, pl.ds(k * T, n * T)], stage.at[pl.ds(k * T, n * T)], load.at[k])
+
+    fetch_len = pltpu.make_async_copy(len_ref, number, load.at[2])
     fetch_len.start()
-    for k in range(chunks):
+    for k in range(2):
         fetch(k).start()
     fetch_len.wait()
     mine = number[0]
@@ -106,8 +107,9 @@
     token = lax.broadcasted_iota(jnp.int32, (T, 1), 0)
 
     def scale(k, first):
-        fetch(k).wait()
-        values = stage[k].astype(f32)
+        if k < 2:
+            fetch(k).wait()
+        values = stage[k * T:(k + 1) * T].astype(f32)
         unit = values * (1.0 / jnp.sqrt(jnp.sum(values * values, axis=1, keepdims=True) + 1e-06))
         first = unit[0:1] if first is None else first
         own[0, k * T:(k + 1) * T] = jnp.where(token + k * T < mine, unit, first).astype(own.dtype)
@@ -523,7 +525,7 @@
         in_specs=[away, pl.BlockSpec(memory_space=pltpu.HBM)],
         out_specs=vmem,
         scratch_shapes=[
-            pltpu.VMEM((chunks, T, width), jnp.bfloat16),
+            pltpu.VMEM((length, width), jnp.bfloat16),
             pltpu.VMEM((2, length, width), jnp.bfloat16),
             pltpu.VMEM((chunks, 2, T, width), jnp.bfloat16),
             pltpu.VMEM((chunks, 2, T, width), jnp.bfloat16),
@@ -534,7 +536,7 @@
             pltpu.VMEM((chunks, 4, 8, 2 * T), jnp.float32),
             pltpu.VMEM((slots, T), jnp.float32),
             pltpu.VMEM((4, slots, T), jnp.float32),
-            dma((chunks + 1,)), dma((TURNS,)), dma(()), dma((2,)), dma(()), dma((chunks,)),
+            dma((3,)), dma((TURNS,)), dma(()), dma((2,)), dma(()), dma((chunks,)),
             dma((chunks,)), dma((count,)), dma((many,)), dma((chunks,)), dma(()),
             dma(()), dma((5,)), dma(()), dma((4,)),
         ],

time: 37.1 us -> 37.2 us (level)
  no operation moved by 1% of the time
where the time goes in v6:
time: 37.2 us; the launch traced here: 37 us
  Pallas kernels  35.7 us (96%)
  between operations  1.28 us (3%)
    pallas_call x1, Pallas kernels, fused(): pl.pallas_call(functools.partial(kernel, slots // 2, slots), out_shape=pl...  35.2 us

profile of v6, /device:TPU:0, one launch (start us, length us, event | category | flops | bytes accessed | tf_op | source)
XLA Modules:
  0.0 37.0 jit_solution(8244633595885285010)
XLA Ops:
  1.3 35.2 %shard_map.41.found_ref = f32[8,128]{1,0:T(8,128)S(1)} custom-call(bf16[1,512,1024]{2,1,0:T(8,128)(2,1)} %emb_ref.1, s32[1]{0:T(128)S(6)} %copy.4.len_ref), custom_call_target="tpu_custom_call" | custom-call | tf_op jit(solution)/shard_map/pallas_call | solution.py:522
  36.5 0.5 %shard_map.42 = (f32[1,8]{1,0:T(1,128)}, f32[1,1]{1,0:T(1,128)}) custom-call(f32[8,128]{1,0:T(8,128)S(1)} %shard_map.41.found_ref), custom_call_target="tpu_custom_call" | custom-call | tf_op jit(solution)/shard_map/pallas_call | solution.py:545

commit v7 on v6

--- a/solution.py
+++ b/solution.py
@@ -10,11 +10,11 @@
 MESH = pl.DeviceIdType.MESH
 T = 128
 PIECE = 64
-FIRST = (16, 16, 32)
-DIRECT = (16, 48, 48, 64)
+FIRST = (16, 48)
+DIRECT = (32, 48, 48, 48)
 AHEAD = 2
-MORE = 4
-HOP = (4, 3, 3, 2)
+MORE = 3
+HOP = (3, 3, 3, 3)
 WINDOW = (256, 192, 192, 128)
 TURNS = 4
 

time: 37.2 us -> 37.1 us (level)
  no operation moved by 1% of the time
where the time goes in v7:
time: 37.1 us; the launch traced here: 37 us
  Pallas kernels  35.7 us (96%)
  between operations  1.28 us (3%)
    pallas_call x1, Pallas kernels, fused(): pl.pallas_call(functools.partial(kernel, slots // 2, slots), out_shape=pl...  35.2 us

profile of v7, /device:TPU:0, one launch (start us, length us, event | category | flops | bytes accessed | tf_op | source)
XLA Modules:
  0.0 37.0 jit_solution(8194426128510028801)
XLA Ops:
  1.3 35.2 %shard_map.41.found_ref = f32[8,128]{1,0:T(8,128)S(1)} custom-call(bf16[1,512,1024]{2,1,0:T(8,128)(2,1)} %emb_ref.1, s32[1]{0:T(128)S(6)} %copy.4.len_ref), custom_call_target="tpu_custom_call" | custom-call | tf_op jit(solution)/shard_map/pallas_call | solution.py:522
  36.4 0.5 %shard_map.42 = (f32[1,8]{1,0:T(1,128)}, f32[1,1]{1,0:T(1,128)}) custom-call(f32[8,128]{1,0:T(8,128)S(1)} %shard_map.41.found_ref), custom_call_target="tpu_custom_call" | custom-call | tf_op jit(solution)/shard_map/pallas_call | solution.py:545
